TPU v7x, 32 devices: a whole 2x2x4 slice. The times are simulated.
32 devices in a mesh: dp: 4 (over z), row: 2 (over x), col: 4 (over y, core).
Axes of the slice: x: 2, y: 2, z: 4, core: 2. Of those that a mesh axis runs over, the one named last changes fastest.
Arguments:
- tokens: bfloat16 [768, 16384], P('row', ('dp', 'col')), may hold values from -6 to 6
- ln_gain: float32 [768], P('row'), may hold values from 0.5 to 1.5
- ln_bias: float32 [768], P('row'), may hold values from -0.3 to 0.3
- qkv_weight: bfloat16 [768, 3, 768], P('row', None, 'col'), may hold values from -0.21875 to 0.21875
- out_weight: bfloat16 [768, 768], P('col', 'row'), may hold values from -6 to 6
- up_weight: bfloat16 [768, 3072], P('row', 'col'), may hold values from -0.21875 to 0.21875
- down_weight: bfloat16 [768, 3072], P('row', 'col'), may hold values from -0.21875 to 0.21875
- mod_weight: bfloat16 [3, 768, 768], P(None, 'row'), may hold values from -0.109375 to 0.109375
- timestep: int32 [8], replicated, may hold values from 0 to 999
- block_size: int32 [8], replicated, may hold values from 32 to 256, as said below
- cotangent: bfloat16 [768, 16384], P('row', ('dp', 'col')), may hold values from -6 to 6
Outputs:
- output: bfloat16 [768, 16384], P('row', ('dp', 'col'))
- tokens_grad: float32 [768, 16384], P('row', ('dp', 'col'))
- ln_gain_grad: float32 [768], P('row')
- ln_bias_grad: float32 [768], P('row')
- qkv_grad: float32 [768, 3, 768], P('row', None, 'col')
- out_grad: float32 [768, 768], P('col', 'row')
- up_grad: float32 [768, 3072], P('row', 'col')
- down_grad: float32 [768, 3072], P('row', 'col')
- mod_grad: float32 [3, 768, 768], P(None, 'row')
Inputs may be any that keep to these rules, and one draw needn't show every extreme that they name: `block_size`: each entry is 256 halved zero to three times; some sequence has 256.
All inputs are finite; a program needn't handle non-finite values.
Results may differ from a plain program's by a relative error of at most 0.02.
Values may be sent and summed in bfloat16 or wider, within the bound.
No kernel may reach another device: no remote copies, remote signals or barrier semaphores. Data moves between devices by JAX's collectives and lax.ppermute only.
A program may use at most 256 MiB of HBM per device.

v0:
```python
from functools import partial
import math
import jax
import jax.numpy as jnp
from jax import lax
from jax.sharding import PartitionSpec as P

HEAD_DIM = 64
LENGTH = 2048
EPSILON = 1e-05
HIGH = lax.Precision.HIGHEST


def time_embed(steps_in, width_all):
    half_width = width_all // 2
    frequency = jnp.exp(-math.log(10000.0) * jnp.arange(half_width, dtype=jnp.float32) / half_width)
    angles = steps_in.astype(jnp.float32)[:, None] * frequency[None, :]
    return jnp.concatenate([jnp.sin(angles), jnp.cos(angles)], axis=1)


def rope_tables(length, head_width):
    half_dim = head_width // 2
    frequency = jnp.exp(-math.log(10000.0) * jnp.arange(half_dim, dtype=jnp.float32) / half_dim)
    angles = jnp.arange(length, dtype=jnp.float32)[:, None] * frequency[None, :]
    return (jnp.cos(angles), jnp.sin(angles))


def rotate(vector, cosine, sine_tab):
    half_dim = vector.shape[-1] // 2
    front_half, back_half = (vector[..., :half_dim], vector[..., half_dim:])
    return jnp.concatenate(
        [front_half * cosine - back_half * sine_tab, back_half * cosine + front_half * sine_tab],
        axis=-1,
    )


def unrotate(grads_in, cosine, sine_tab):
    half_dim = grads_in.shape[-1] // 2
    front_half, back_half = (grads_in[..., :half_dim], grads_in[..., half_dim:])
    return jnp.concatenate(
        [front_half * cosine + back_half * sine_tab, back_half * cosine - front_half * sine_tab],
        axis=-1,
    )


def token_totals(first_terms, second_terms):
    return lax.psum((jnp.sum(first_terms, axis=1), jnp.sum(second_terms, axis=1)), "row")


def norm_forward(values, width_all):
    sum_plain, sum_square = token_totals(values, values * values)
    mean_row = sum_plain / width_all
    inv_std = lax.rsqrt(sum_square / width_all - mean_row * mean_row + EPSILON)
    return ((values - mean_row[:, None]) * inv_std[:, None], inv_std)


def norm_backward(grad_norm, normed, inv_std, width_all):
    sum_plain, sum_cross = token_totals(grad_norm, grad_norm * normed)
    return inv_std[:, None] * (
        grad_norm - sum_plain[:, None] / width_all - normed * (sum_cross[:, None] / width_all)
    )


def gather_col(local_part):
    return lax.all_gather(local_part, "col", axis=0, tiled=True)


def gather_rows(local_part):
    return lax.all_gather(local_part, "row", axis=0, tiled=True)


def row_product(gathered, tile_part):
    return lax.psum_scatter(
        jnp.dot(gathered, tile_part, preferred_element_type=jnp.float32),
        "row",
        scatter_dimension=0,
        tiled=True,
    )


def col_product(gathered, tile_part):
    return lax.psum_scatter(
        jnp.dot(gathered, tile_part, preferred_element_type=jnp.float32),
        "col",
        scatter_dimension=0,
        tiled=True,
    )


def block_index(block_lens, length):
    positions = jnp.arange(length, dtype=jnp.int32)
    return positions[None, :] // block_lens[:, None]


def masked_scores(query_part, key_rows, key_block, query_block, score_scale):
    scores = (
        jnp.einsum("sqhd,skhd->shqk", query_part, key_rows, preferred_element_type=jnp.float32)
        * score_scale
    )
    visible = key_block[:, None, None, :] <= query_block[:, None, :, None]
    return jnp.where(visible, scores, -1e30)


def attend_forward(queries, key_rows, value_rows, block_lens):
    length = queries.shape[1]
    rows_per = min(512, length)
    score_scale = queries.shape[3] ** (-0.5)
    key_block = block_index(block_lens, length)

    def one_block(offset):
        query_part = lax.dynamic_slice_in_dim(queries, offset, rows_per, 1)
        query_block = lax.dynamic_slice_in_dim(key_block, offset, rows_per, 1)
        scores = masked_scores(query_part, key_rows, key_block, query_block, score_scale)
        row_top = jnp.max(scores, axis=-1, keepdims=True)
        raised = jnp.exp(scores - row_top)
        row_total = jnp.sum(raised, axis=-1, keepdims=True)
        weights = (raised / row_total).astype(jnp.bfloat16)
        block_out = jnp.einsum(
            "shqk,skhd->sqhd", weights, value_rows, preferred_element_type=jnp.float32
        )
        return (block_out, row_top[..., 0] + jnp.log(row_total[..., 0]))

    offsets = jnp.arange(0, length, rows_per, dtype=jnp.int32)
    block_outs, log_totals = lax.map(one_block, offsets)
    return (jnp.moveaxis(block_outs, 0, 1).reshape(queries.shape), log_totals)


def attend_backward(queries, key_rows, value_rows, grad_mixed, log_totals, block_lens):
    length = queries.shape[1]
    rows_per = min(512, length)
    score_scale = queries.shape[3] ** (-0.5)
    key_block = block_index(block_lens, length)

    def one_block(running, element):
        grad_keys, grad_values = running
        offset, log_part = element
        query_part = lax.dynamic_slice_in_dim(queries, offset, rows_per, 1)
        grad_part = lax.dynamic_slice_in_dim(grad_mixed, offset, rows_per, 1)
        query_block = lax.dynamic_slice_in_dim(key_block, offset, rows_per, 1)
        scores = masked_scores(query_part, key_rows, key_block, query_block, score_scale)
        weights = jnp.exp(scores - log_part[..., None])
        grad_weights = jnp.einsum(
            "sqhd,skhd->shqk", grad_part, value_rows, preferred_element_type=jnp.float32
        )
        grad_scores = weights * (
            grad_weights - jnp.sum(weights * grad_weights, axis=-1, keepdims=True)
        )
        grad_scores = grad_scores.astype(jnp.bfloat16)
        grad_query = (
            jnp.einsum("shqk,skhd->sqhd", grad_scores, key_rows, preferred_element_type=jnp.float32)
            * score_scale
        )
        grad_keys = (
            grad_keys
            + jnp.einsum(
                "shqk,sqhd->skhd", grad_scores, query_part, preferred_element_type=jnp.float32
            )
            * score_scale
        )
        grad_values = grad_values + jnp.einsum(
            "shqk,sqhd->skhd",
            weights.astype(jnp.bfloat16),
            grad_part,
            preferred_element_type=jnp.float32,
        )
        return ((grad_keys, grad_values), grad_query)

    offsets = jnp.arange(0, length, rows_per, dtype=jnp.int32)
    zero_grads = jnp.zeros(queries.shape, jnp.float32)
    (grad_keys, grad_values), grad_queries = lax.scan(
        one_block, (zero_grads, zero_grads), (offsets, log_totals)
    )
    return (jnp.moveaxis(grad_queries, 0, 1).reshape(queries.shape), grad_keys, grad_values)


def local(
    tokens,
    ln_gain,
    ln_bias,
    qkv_weight,
    out_weight,
    up_weight,
    down_weight,
    mod_weight,
    timestep,
    block_size,
    cotangent,
):
    n_row = lax.axis_size("row")
    n_col = lax.axis_size("col")
    width_all = mod_weight.shape[2]
    feat_local, local_tokens = tokens.shape
    group_tokens = local_tokens * n_col
    seq_here = group_tokens // n_row // LENGTH
    heads_here = qkv_weight.shape[2] // HEAD_DIM
    group_index = lax.axis_index("dp")
    first_token = group_index * group_tokens + lax.axis_index("col") * local_tokens
    seq_count = max(1, local_tokens // LENGTH)
    token_span = local_tokens // seq_count
    steps_here = lax.dynamic_slice_in_dim(timestep, first_token // LENGTH, seq_count, 0)
    embedded = time_embed(steps_here, width_all)
    modulation = jnp.einsum("nd,ked->kne", embedded, mod_weight.astype(jnp.float32), precision=HIGH)

    def per_token(table):
        return jnp.broadcast_to(table[:, None, :], (seq_count, token_span, feat_local)).reshape(
            local_tokens, feat_local
        )

    def per_sequence(values):
        return jnp.sum(values.reshape(seq_count, token_span, feat_local), axis=1)

    scale_tok = per_token(modulation[0])
    shift_tok = per_token(modulation[1])
    gate_tok = per_token(modulation[2])
    resid = tokens.astype(jnp.float32).T
    norm_one, inv_one = norm_forward(resid, width_all)
    act_one = (norm_one * ln_gain + ln_bias).astype(jnp.bfloat16)
    act_one_all = gather_col(act_one)
    qkv_tile = qkv_weight.reshape(feat_local, -1)
    projected = row_product(act_one_all, qkv_tile).reshape(
        seq_here, LENGTH, 3, heads_here, HEAD_DIM
    )
    cosine, sine_tab = rope_tables(LENGTH, HEAD_DIM)
    cosine = cosine[None, :, None, :]
    sine_tab = sine_tab[None, :, None, :]
    queries = rotate(projected[:, :, 0], cosine, sine_tab).astype(jnp.bfloat16)
    key_rows = rotate(projected[:, :, 1], cosine, sine_tab).astype(jnp.bfloat16)
    value_rows = projected[:, :, 2].astype(jnp.bfloat16)
    seq_first = (group_index * n_row + lax.axis_index("row")) * seq_here
    block_lens = lax.dynamic_slice_in_dim(block_size, seq_first, seq_here, 0)
    attended, log_totals = attend_forward(queries, key_rows, value_rows, block_lens)
    attn_mix = attended.reshape(seq_here * LENGTH, heads_here * HEAD_DIM).astype(jnp.bfloat16)
    attn_mix_all = gather_rows(attn_mix)
    branch_one = col_product(attn_mix_all, out_weight)
    hidden_one = resid + branch_one
    norm_two, inv_two = norm_forward(hidden_one, width_all)
    act_two = (norm_two * (1.0 + scale_tok) + shift_tok).astype(jnp.bfloat16)
    act_two_all = gather_col(act_two)
    pre_act = row_product(act_two_all, up_weight)
    gelu_out = jax.nn.gelu(pre_act, approximate=True).astype(jnp.bfloat16)
    gelu_all = gather_rows(gelu_out)
    branch_two = col_product(gelu_all, down_weight.T)
    result = hidden_one + (1.0 + gate_tok) * branch_two
    grad_out = cotangent.astype(jnp.float32).T
    gate_term = grad_out * branch_two
    grad_two = (grad_out * (1.0 + gate_tok)).astype(jnp.bfloat16)
    grad_two_all = gather_col(grad_two)
    grad_gelu = row_product(grad_two_all, down_weight)
    down_grad = jnp.einsum("td,tf->df", grad_two_all, gelu_all, preferred_element_type=jnp.float32)
    _, gelu_pull = jax.vjp(partial(jax.nn.gelu, approximate=True), pre_act)
    grad_pre = gelu_pull(grad_gelu)[0].astype(jnp.bfloat16)
    grad_pre_all = gather_rows(grad_pre)
    grad_act_two = col_product(grad_pre_all, up_weight.T)
    up_grad = jnp.einsum("td,tf->df", act_two_all, grad_pre_all, preferred_element_type=jnp.float32)
    scale_term = grad_act_two * norm_two
    grad_hidden = grad_out + norm_backward(
        grad_act_two * (1.0 + scale_tok), norm_two, inv_two, width_all
    )
    grad_one = grad_hidden.astype(jnp.bfloat16)
    grad_one_all = gather_col(grad_one)
    grad_attn = row_product(grad_one_all, out_weight.T)
    out_grad = jnp.einsum(
        "tc,td->cd", attn_mix_all, grad_one_all, preferred_element_type=jnp.float32
    )
    grad_attn = grad_attn.astype(jnp.bfloat16).reshape(seq_here, LENGTH, heads_here, HEAD_DIM)
    grad_queries, grad_keys, grad_values = attend_backward(
        queries, key_rows, value_rows, grad_attn, log_totals, block_lens
    )
    grad_queries = unrotate(grad_queries, cosine, sine_tab)
    grad_keys = unrotate(grad_keys, cosine, sine_tab)
    grad_projected = jnp.stack([grad_queries, grad_keys, grad_values], axis=2).astype(jnp.bfloat16)
    grad_projected = grad_projected.reshape(seq_here * LENGTH, 3 * heads_here * HEAD_DIM)
    grad_proj_all = gather_rows(grad_projected)
    grad_act_one = col_product(grad_proj_all, qkv_tile.T)
    qkv_grad = jnp.einsum(
        "td,tk->dk", act_one_all, grad_proj_all, preferred_element_type=jnp.float32
    ).reshape(qkv_weight.shape)
    gain_part = jnp.sum(grad_act_one * norm_one, axis=0)
    bias_part = jnp.sum(grad_act_one, axis=0)
    tokens_grad = grad_hidden + norm_backward(grad_act_one * ln_gain, norm_one, inv_one, width_all)
    grad_mod = jnp.stack(
        [per_sequence(scale_term), per_sequence(grad_act_two), per_sequence(gate_term)]
    )
    mod_part = jnp.einsum("nd,kne->ked", embedded, grad_mod, precision=HIGH)
    gain_grad, bias_grad, mod_grad = (
        lax.psum(gain_part.astype(jnp.bfloat16), ("dp", "col")).astype(jnp.float32),
        lax.psum(bias_part.astype(jnp.bfloat16), ("dp", "col")).astype(jnp.float32),
        lax.psum(mod_part.astype(jnp.bfloat16), ("dp", "col")).astype(jnp.float32),
    )
    qkv_grad, out_grad, up_grad, down_grad = (
        lax.psum(qkv_grad.astype(jnp.bfloat16), "dp").astype(jnp.float32),
        lax.psum(out_grad.astype(jnp.bfloat16), "dp").astype(jnp.float32),
        lax.psum(up_grad.astype(jnp.bfloat16), "dp").astype(jnp.float32),
        lax.psum(down_grad.astype(jnp.bfloat16), "dp").astype(jnp.float32),
    )
    return (
        result.astype(jnp.bfloat16).T,
        tokens_grad.T,
        gain_grad,
        bias_grad,
        qkv_grad,
        out_grad,
        up_grad,
        down_grad,
        mod_grad,
    )


def solution(mesh):
    placed = (
        P("row", ("dp", "col")),
        P("row"),
        P("row"),
        P("row", None, "col"),
        P("col", "row"),
        P("row", "col"),
        P("row", "col"),
        P(None, "row", None),
        P(),
        P(),
        P("row", ("dp", "col")),
    )
    return jax.shard_map(
        local,
        mesh=mesh,
        in_specs=placed,
        out_specs=(
            P("row", ("dp", "col")),
            P("row", ("dp", "col")),
            P("row"),
            P("row"),
            P("row", None, "col"),
            P("col", "row"),
            P("row", "col"),
            P("row", "col"),
            P(None, "row", None),
        ),
        check_vma=False,
    )
```

profile of v0, /device:TPU:0, one launch (start us, length us, event | category | flops | bytes accessed | tf_op | source)
XLA Modules:
  0.0 1632.1 jit_solution(8770067134209926731)
XLA Ops:
  17.3 30.4 %all-gather.9.cloned.1.call-done = bf16[4096,384]{1,0:T(8,128)(2,1)} async-done(((bf16[1024,384]{1,0:T(8,128)(2,1)}), bf16[4096,384]{1,0:T(8,128)(2,1)}) %all-gather.9.cloned.1.call-update) | async-done | bytes 3145744 | tf_op jit(solution)/shard_map/all_gather | solution.py:65
  58.9 106.6 %reduce-scatter.9.cloned.1.call-done = f32[2048,576]{0,1:T(8,128)} async-done(((f32[4096,576]{0,1:T(8,128)}), f32[2048,576]{0,1:T(8,128)}) %reduce-scatter.9.cloned.1.call-update) | async-done | bytes 4718608 | tf_op jit(solution)/shard_map/reduce_scatter | solution.py:73
  170.5 98.7 %while.27 = (s32[]{:T(128)}, bf16[4,1,512,3,64]{2,4,3,1,0:T(8,128)(2,1)}, f32[4,1,3,512]{3,2,1,0:T(4,128)S(1)}, s32[1,2048]{1,0:T(1,128)S(1)}, s32[4]{0:T(128)S(...) while((s32[]{:T(128)}, ...), condition=%wide.region_8.10_spmd, body=%wide.region_5.9_spmd.sunk | while | flops 844102144 | bytes 50471144 | solution.py:124
  272.4 27.1 %all-gather.11.cloned.1.call-done = bf16[4096,192]{0,1:T(8,128)(2,1)} async-done(((bf16[2048,192]{0,1:T(8,128)(2,1)}), bf16[4096,192]{0,1:T(8,128)(2,1)}) %all-gather.11.cloned.1.call-update) | async-done | bytes 1572880 | tf_op jit(solution)/shard_map/all_gather | solution.py:69
  311.7 52.2 %reduce-scatter.11.cloned.1.call-done = f32[1024,384]{1,0:T(8,128)} async-done(((f32[4096,384]{1,0:T(8,128)}), f32[1024,384]{1,0:T(8,128)}) %reduce-scatter.11.cloned.1.call-update) | async-done | bytes 1572880 | tf_op jit(solution)/shard_map/reduce_scatter | solution.py:82
  374.6 19.8 %all-gather.17.cloned.1.call-done = bf16[4096,384]{1,0:T(8,128)(2,1)} async-done(((bf16[1024,384]{1,0:T(8,128)(2,1)}), bf16[4096,384]{1,0:T(8,128)(2,1)}) %all-gather.17.cloned.1.call-update) | async-done | bytes 3145744 | tf_op jit(solution)/shard_map/all_gather | solution.py:65
  394.4 10.4 fusion.89
  404.9 20.0 %all-gather.13.cloned.1.call-done = bf16[4096,384]{1,0:T(8,128)(2,1)} async-done(((bf16[1024,384]{1,0:T(8,128)(2,1)}), bf16[4096,384]{1,0:T(8,128)(2,1)}) %all-gather.13.cloned.1.call-update) | async-done | bytes 3145744 | tf_op jit(solution)/shard_map/all_gather | solution.py:65
  425.0 10.5 fusion.87
  436.0 135.8 %reduce-scatter.17.cloned.1.call-done = f32[2048,768]{1,0:T(8,128)} async-done(((f32[4096,768]{1,0:T(8,128)}), f32[2048,768]{1,0:T(8,128)}) %reduce-scatter.17.cloned.1.call-update) | async-done | bytes 6291472 | tf_op jit(solution)/shard_map/reduce_scatter | solution.py:73
  571.8 146.9 %reduce-scatter.13.cloned.1.call-done = f32[2048,768]{1,0:T(8,128)} async-done(((f32[4096,768]{1,0:T(8,128)}), f32[2048,768]{1,0:T(8,128)}) %reduce-scatter.13.cloned.1.call-update) | async-done | bytes 6291472 | tf_op jit(solution)/shard_map/reduce_scatter | solution.py:73
  718.7 9.0 fusion.51
  728.4 79.9 %all-gather.19.cloned.1.call-done = bf16[4096,768]{1,0:T(8,128)(2,1)} async-done(((bf16[2048,768]{1,0:T(8,128)(2,1)}), bf16[4096,768]{1,0:T(8,128)(2,1)}) %all-gather.19.cloned.1.call-update) | async-done | bytes 6291472 | tf_op jit(solution)/shard_map/all_gather | solution.py:69
  808.3 9.4 fusion.90
  817.7 72.3 %all-gather.15.cloned.1.call-done = bf16[4096,768]{1,0:T(8,128)(2,1)} async-done(((bf16[2048,768]{1,0:T(8,128)(2,1)}), bf16[4096,768]{1,0:T(8,128)(2,1)}) %all-gather.15.cloned.1.call-update) | async-done | bytes 6291472 | tf_op jit(solution)/shard_map/all_gather | solution.py:69
  890.0 9.4 fusion.88
  899.5 52.0 %reduce-scatter.19.cloned.1.call-done = f32[1024,384]{1,0:T(8,128)} async-done(((f32[4096,384]{1,0:T(8,128)}), f32[1024,384]{1,0:T(8,128)}) %reduce-scatter.19.cloned.1.call-update) | async-done | bytes 1572880 | tf_op jit(solution)/shard_map/reduce_scatter | solution.py:82
  959.2 53.5 %reduce-scatter.15.cloned.1.call-done = f32[1024,384]{1,0:T(8,128)} async-done(((f32[4096,384]{1,0:T(8,128)}), f32[1024,384]{1,0:T(8,128)}) %reduce-scatter.15.cloned.1.call-update) | async-done | bytes 1572880 | tf_op jit(solution)/shard_map/reduce_scatter | solution.py:82
  1017.0 28.6 %all-gather.21.cloned.1.call-done = bf16[4096,384]{1,0:T(8,128)(2,1)} async-done(((bf16[1024,384]{1,0:T(8,128)(2,1)}), bf16[4096,384]{1,0:T(8,128)(2,1)}) %all-gather.21.cloned.1.call-update) | async-done | bytes 3145744 | tf_op jit(solution)/shard_map/all_gather | solution.py:65
  1050.5 43.5 %reduce-scatter.21.cloned.1.call-done = f32[2048,192]{0,1:T(8,128)} async-done(((f32[4096,192]{0,1:T(8,128)}), f32[2048,192]{0,1:T(8,128)}) %reduce-scatter.21.cloned.1.call-update) | async-done | bytes 1572880 | tf_op jit(solution)/shard_map/reduce_scatter | solution.py:73
  1096.4 173.6 %while.28 = (s32[]{:T(128)}, f32[1,2048,3,64]{1,3,2,0:T(8,128)}, f32[1,2048,3,64]{1,3,2,0:T(8,128)}, f32[4,1,512,3,64]{2,0,4,3,1:T(4,128)}, s32[4]{0:T(128)S(1)}...) while((s32[]{:T(128)}, f32[1,2048,3,64]{1,3,2,0:T(8,128)}, ...), condition=%wide.region_25.27_spmd.clone, body=%wide.region_23.26_spmd.clone.sunk | while | flops 2063563264 | bytes 151970208 | solution.py:170
  1130.4 8.6 dynamic_update_slice.19
  1174.1 8.6 dynamic_update_slice.19
  1217.7 8.6 dynamic_update_slice.19
  1261.2 8.6 dynamic_update_slice.19
  1284.8 7.1 convolution_convert_fusion
  1297.5 42.6 %all-gather.23.cloned.1.call-done = bf16[4096,576]{0,1:T(8,128)(2,1)} async-done(((bf16[2048,576]{0,1:T(8,128)(2,1)}), bf16[4096,576]{0,1:T(8,128)(2,1)}) %all-gather.23.cloned.1.call-update) | async-done | bytes 4718608 | tf_op jit(solution)/shard_map/all_gather | solution.py:69
  1347.1 8.4 fusion.92
  1357.9 82.4 %all-reduce.9.cloned.1.call-done = bf16[3,384,768]{2,1,0:T(8,128)(2,1)} async-done(((bf16[3,384,768]{2,1,0:T(8,128)(2,1)}), bf16[3,384,768]{2,1,0:T(8,128)(2,1)}) %all-reduce.9.cloned.1.call-update) | async-done | bytes 1769488 | tf_op jit(solution)/shard_map/psum | solution.py:288
  1443.8 73.8 %all-reduce.11.cloned.1.call-done = (bf16[384,3,192]{0,2,1:T(8,128)(2,1)}, bf16[192,384]{1,0:T(8,128)(2,1)}, bf16[384,768]{1,0:T(8,128)(2,1)}, bf16[384,768]{1,0:T(8,128)(2,1)}) async-done(((bf16[384,3,192]{0,2,1:T(8,128)(2,1)}, bf16[192,384]{1,0:T(8,128)(2,1)}, bf16[384,768]{1,0:T(8,128)(2,1)}, bf16[384,768]{1,0:T(8,128)(2,1)}), (bf16[384,3,192]{0,2,1:T(8,128)(2,1)}, bf16[192,384]{1,0:T(8,128)(2,1)}, ...) | async-done | bytes 1769488 | tf_op jit(solution)/shard_map/psum | solution.py:291
  1524.6 53.3 %reduce-scatter.23.cloned.1.call-done = f32[1024,384]{1,0:T(8,128)} async-done(((f32[4096,384]{1,0:T(8,128)}), f32[1024,384]{1,0:T(8,128)}) %reduce-scatter.23.cloned.1.call-update) | async-done | bytes 1572880 | tf_op jit(solution)/shard_map/reduce_scatter | solution.py:82
  1580.2 32.1 %all-reduce.4 = (bf16[384]{0:T(512)(128)(2,1)S(1)}, bf16[384]{0:T(512)(128)(2,1)S(1)}) all-reduce(bf16[384]{0:T(512)(128)(2,1)S(1)} %get-tuple-element.173, bf16[384]{0:T(512)(128)(2,1)S(1)} %get-tuple-element.178), channel_id=1, replica_groups=mesh['dp'=4,'row'=2,'col'=4] {'dp','col'}, use_global_device_ids=true, to_apply=%region_32.34 | all-reduce | flops 768 | bytes 3072 | tf_op jit(solution)/shard_map/psum | solution.py:286
  (319 shorter events, 347.5 us)
Async XLA Ops:
  7.2 300.2 %copy-start = (bf16[3,384,768]{2,1,0:T(8,128)(2,1)S(1)}, bf16[3,384,768]{2,1,0:T(8,128)(2,1)}, u32[]{:S(2)}) copy-start(bf16[3,384,768]{2,1,0:T(8,128)(2,1)} %param.24) | copy-start | bytes 5308420
  7.2 40.5 %copy-start.28 = (bf16[384,3,192]{0,2,1:T(8,128)(2,1)S(1)}, bf16[384,3,192]{0,2,1:T(8,128)(2,1)}, u32[]{:S(2)}) copy-start(bf16[384,3,192]{0,2,1:T(8,128)(2,1)} %param.20) | copy-start | bytes 1327108
  7.2 40.4 %all-gather.9.cloned.1.call-start = ((), (), s32[]{:S(2)}) async-start(), calls=%async_computation.8 | async-start | bytes 3932160 | tf_op jit(solution)/shard_map/all_gather | solution.py:65
  8.9 45.7 %copy-start.9 = (bf16[384,1024]{0,1:T(8,128)(2,1)}, bf16[384,1024]{0,1:T(8,128)(2,1)S(1)}, u32[]{:S(2)}) copy-start(bf16[384,1024]{0,1:T(8,128)(2,1)S(1)} %copy.24) | copy-start | bytes 2359300
  17.2 148.2 %reduce-scatter.9.cloned.1.call-start = ((), (), s32[]{:S(2)}) async-start(), calls=%async_computation.9 | async-start | bytes 14155776 | tf_op jit(solution)/shard_map/reduce_scatter | solution.py:73
  54.7 244.8 %all-gather.11.cloned.1.call-start = ((), (), s32[]{:S(2)}) async-start(), calls=%async_computation.10 | async-start | bytes 2359296 | tf_op jit(solution)/shard_map/all_gather | solution.py:69
  58.9 110.2 %copy-start.18 = (f32[2048,32]{0,1:T(8,128)}, f32[2048,32]{0,1:T(8,128)S(1)}, u32[]{:S(2)}) copy-start(f32[2048,32]{0,1:T(8,128)S(1)} %get-tuple-element.267) | copy-start | bytes 786436
  58.9 110.2 %copy-start.20 = (f32[2048,32]{0,1:T(8,128)}, f32[2048,32]{0,1:T(8,128)S(1)}, u32[]{:S(2)}) copy-start(f32[2048,32]{0,1:T(8,128)S(1)} %get-tuple-element.268) | copy-start | bytes 786436
  272.2 91.8 %reduce-scatter.11.cloned.1.call-start = ((), (), s32[]{:S(2)}) async-start(), calls=%async_computation.11 | async-start | bytes 7864320 | tf_op jit(solution)/shard_map/reduce_scatter | solution.py:82
  304.9 89.5 %all-gather.17.cloned.1.call-start = ((), (), s32[]{:S(2)}) async-start(), calls=%async_computation.16 | async-start | bytes 3932160 | tf_op jit(solution)/shard_map/all_gather | solution.py:65
  308.9 55.0 %copy-start.10 = (bf16[384,1024]{0,1:T(8,128)(2,1)S(1)}, bf16[384,1024]{0,1:T(8,128)(2,1)}, u32[]{:S(2)}) copy-start(bf16[384,1024]{0,1:T(8,128)(2,1)} %copy-done.9) | copy-start | bytes 2359300
  310.5 56.1 %copy-start.16 = (bf16[384,1024]{0,1:T(8,128)(2,1)}, bf16[384,1024]{0,1:T(8,128)(2,1)S(1)}, u32[]{:S(2)}) copy-start(bf16[384,1024]{0,1:T(8,128)(2,1)S(1)} %copy.26) | copy-start | bytes 2359300
  311.6 113.3 %all-gather.13.cloned.1.call-start = ((), (), s32[]{:S(2)}) async-start(), calls=%async_computation.12 | async-start | bytes 3932160 | tf_op jit(solution)/shard_map/all_gather | solution.py:65
  374.5 197.3 %reduce-scatter.17.cloned.1.call-start = ((), (), s32[]{:S(2)}) async-start(), calls=%async_computation.17 | async-start | bytes 18874368 | tf_op jit(solution)/shard_map/reduce_scatter | solution.py:73
  404.9 313.9 %reduce-scatter.13.cloned.1.call-start = ((), (), s32[]{:S(2)}) async-start(), calls=%async_computation.13 | async-start | bytes 18874368 | tf_op jit(solution)/shard_map/reduce_scatter | solution.py:73
  435.5 372.7 %all-gather.19.cloned.1.call-start = ((), (), s32[]{:S(2)}) async-start(), calls=%async_computation.18 | async-start | bytes 9437184 | tf_op jit(solution)/shard_map/all_gather | solution.py:69
  727.8 162.3 %all-gather.15.cloned.1.call-start = ((), (), s32[]{:S(2)}) async-start(), calls=%async_computation.14 | async-start | bytes 9437184 | tf_op jit(solution)/shard_map/all_gather | solution.py:69
  728.3 223.1 %reduce-scatter.19.cloned.1.call-start = ((), (), s32[]{:S(2)}) async-start(), calls=%async_computation.19 | async-start | bytes 7864320 | tf_op jit(solution)/shard_map/reduce_scatter | solution.py:82
  817.6 72.4 %copy-start.25 = (bf16[384,768]{1,0:T(8,128)(2,1)S(1)}, bf16[384,768]{1,0:T(8,128)(2,1)}, u32[]{:S(2)}) copy-start(bf16[384,768]{1,0:T(8,128)(2,1)} %param.23) | copy-start | bytes 1769476
  817.7 195.0 %reduce-scatter.15.cloned.1.call-start = ((), (), s32[]{:S(2)}) async-start(), calls=%async_computation.15 | async-start | bytes 7864320 | tf_op jit(solution)/shard_map/reduce_scatter | solution.py:82
  899.4 52.0 %copy-start.12 = (f32[1024,384]{1,0:T(8,128)S(1)}, f32[1024,384]{1,0:T(8,128)}, u32[]{:S(2)}) copy-start(f32[1024,384]{1,0:T(8,128)} %get-tuple-element.238) | copy-start | bytes 4718596
  899.4 146.2 %all-gather.21.cloned.1.call-start = ((), (), s32[]{:S(2)}) async-start(), calls=%async_computation.20 | async-start | bytes 3932160 | tf_op jit(solution)/shard_map/all_gather | solution.py:65
  1016.9 77.1 %reduce-scatter.21.cloned.1.call-start = ((), (), s32[]{:S(2)}) async-start(), calls=%async_computation.21 | async-start | bytes 4718592 | tf_op jit(solution)/shard_map/reduce_scatter | solution.py:73
  1050.4 289.7 %all-gather.23.cloned.1.call-start = ((), (), s32[]{:S(2)}) async-start(), calls=%async_computation.22 | async-start | bytes 7077888 | tf_op jit(solution)/shard_map/all_gather | solution.py:69
  1277.3 162.9 %all-reduce.9.cloned.1.call-start = ((), (), s32[]{:S(2)}) async-start(), calls=%async_computation.24 | async-start | bytes 3538944 | tf_op jit(solution)/shard_map/psum | solution.py:288
  1293.5 224.1 %all-reduce.11.cloned.1.call-start = ((), (), s32[]{:S(2)}) async-start(), calls=%async_computation.25 | async-start | bytes 3538944 | tf_op jit(solution)/shard_map/psum | solution.py:291
  1297.5 49.7 %copy-start.29 = (bf16[384,3,192]{0,2,1:T(8,128)(2,1)S(1)}, bf16[384,3,192]{0,2,1:T(8,128)(2,1)}, u32[]{:S(2)}) copy-start(bf16[384,3,192]{0,2,1:T(8,128)(2,1)} %param.20) | copy-start | bytes 1327108
  1346.8 231.1 %reduce-scatter.23.cloned.1.call-start = ((), (), s32[]{:S(2)}) async-start(), calls=%async_computation.23 | async-start | bytes 7864320 | tf_op jit(solution)/shard_map/reduce_scatter | solution.py:82
  1443.8 134.1 %copy-start.11 = (bf16[384,1024]{0,1:T(8,128)(2,1)S(1)}, bf16[384,1024]{0,1:T(8,128)(2,1)}, u32[]{:S(2)}) copy-start(bf16[384,1024]{0,1:T(8,128)(2,1)} %copy-done.9) | copy-start | bytes 2359300
  1443.8 134.1 %copy-start.31 = (f32[1024]{0:T(1024)S(1)}, f32[1024]{0:T(1024)}, u32[]{:S(2)}) copy-start(f32[1024]{0:T(1024)} %copy-done.30) | copy-start | bytes 12292
  1443.8 134.1 %copy-start.33 = (f32[1024]{0:T(1024)S(1)}, f32[1024]{0:T(1024)}, u32[]{:S(2)}) copy-start(f32[1024]{0:T(1024)} %copy-done.32) | copy-start | bytes 12292
  1443.8 134.1 %copy-start.35 = (f32[384]{0:T(512)S(1)}, f32[384]{0:T(512)}, u32[]{:S(2)}) copy-start(f32[384]{0:T(512)} %param.18) | copy-start | bytes 4612
  (56 other events, 378.6 us)
Sparse Core Ops, SparseCore 0:
  17.3 30.2 all-gather.8
  54.8 110.6 reduce-scatter.8
  272.3 27.1 all-gather.10
  305.0 58.8 reduce-scatter.10
  365.9 28.4 all-gather.16
  396.4 28.4 all-gather.12
  427.3 144.5 reduce-scatter.16
  574.1 144.5 reduce-scatter.12
  727.9 80.3 all-gather.18
  809.6 80.3 all-gather.14
  892.6 58.8 reduce-scatter.18
  953.8 58.8 reduce-scatter.14
  1017.1 28.5 all-gather.20
  1050.6 43.3 reduce-scatter.20
  1277.4 62.6 all-gather.22
  1343.5 96.7 all-reduce.8
  1443.3 74.3 all-reduce.10
  1520.0 57.8 reduce-scatter.22
where the time goes:
time: 1640 us; the launch traced here: 1630 us
  waiting for transfers between devices  1120 us (68%)
  matrix products  243 us (15%)
  other arithmetic  111 us (7%)
  local copies, waits for them, and re-layouts  68.2 us (4%)
  blocking collectives  53.1 us (3%)
  between operations  16.6 us (1%)
  loops' own time  16.4 us (1%)
    reduce_scatter x4, waiting for transfers between devices, row_product(): lax.psum_scatter(jnp.dot(gathered, tile_part, preferred_element_type=jnp....  433 us
    all_gather x4, waiting for transfers between devices, gather_rows(): return lax.all_gather(local_part, 'row', axis=0, tiled=True)  222 us
    reduce_scatter x4, waiting for transfers between devices, col_product(): lax.psum_scatter(jnp.dot(gathered, tile_part, preferred_element_type=jnp....  211 us
    all_gather x4, waiting for transfers between devices, gather_col(): return lax.all_gather(local_part, 'col', axis=0, tiled=True)  98.9 us
    psum x1, waiting for transfers between devices, local(): lax.psum(mod_part.astype(jnp.bfloat16), ('dp', 'col')).astype(jnp.float32)  82.4 us
    psum x1, waiting for transfers between devices, local(): lax.psum(qkv_grad.astype(jnp.bfloat16), 'dp').astype(jnp.float32)  73.8 us
    dot_general x8, matrix products, masked_scores(): jnp.einsum('sqhd,skhd->shqk', query_part, key_rows, preferred_element_typ...  40.6 us
    dynamic_update_slice x8, local copies, waits for them, and re-layouts, attend_forward(): block_outs, log_totals = lax.map(one_block, offsets)  36.1 us
  transfers between devices with their start and end apart: 18, of which 18 were waited for; matrix products, arithmetic and copies ran while one was open for 6% of the time, Pallas kernels for 0%

commit v1 on v0

--- a/solution.py
+++ b/solution.py
@@ -11,6 +11,28 @@
 HIGH = lax.Precision.HIGHEST
 
 
+def joined_along(parts, dim):
+    parts = jnp.moveaxis(parts, 0, dim)
+    dims = parts.shape
+    return parts.reshape(*dims[:dim], dims[dim] * dims[dim + 1], *dims[dim + 2 :])
+
+
+def collect(value, axis, dim):
+    size = lax.axis_size(axis)
+    pairs = [(i, (i + 1) % size) for i in range(size)]
+    back = [(b, a) for a, b in pairs]
+    lower, upper = ([], [])
+    for step in range(size - 1):
+        if step % 2 == 0:
+            lower.append(lax.ppermute(lower[-1] if lower else value, axis, pairs))
+        else:
+            upper.append(lax.ppermute(upper[-1] if upper else value, axis, back))
+    tiles = jnp.stack([*lower[::-1], value, *upper])
+    shift = lax.axis_index(axis) - len(lower)
+    tiles = tiles[(jnp.arange(size) - shift) % size]
+    return joined_along(tiles, dim)
+
+
 def time_embed(steps_in, width_all):
     half_width = width_all // 2
     frequency = jnp.exp(-math.log(10000.0) * jnp.arange(half_width, dtype=jnp.float32) / half_width)
@@ -62,7 +84,7 @@
 
 
 def gather_col(local_part):
-    return lax.all_gather(local_part, "col", axis=0, tiled=True)
+    return collect(local_part, "col", 0)
 
 
 def gather_rows(local_part):

time: 1640 us -> 1610 us (0.982)
  waiting for transfers between devices: 1120 us -> 1050 us
  local copies, waits for them, and re-layouts: 68.2 us -> 86.7 us
    ppermute x0 -> x12, waiting for transfers between devices: none -> 120 us  [the longest x8 118 us: collect(): lower.append(lax.ppermute(lower[-1] if lower else value, axis, pairs))]
    all_gather x4 -> x0, waiting for transfers between devices: 98.9 us -> none  [gather_col(): return lax.all_gather(local_part, 'col', axis=0, tiled=True)]
    reduce_scatter x4, waiting for transfers between devices: 211 us -> 159 us  [col_product(): lax.psum_scatter(jnp.dot(gathered, tile_part, preferred_element_type=jnp....]
    reduce_scatter x4, waiting for transfers between devices: 433 us -> 390 us  [row_product(): lax.psum_scatter(jnp.dot(gathered, tile_part, preferred_element_type=jnp....]
    gather x0 -> x4, local copies, waits for them, and re-layouts: none -> 18.8 us  [collect(): tiles = tiles[(jnp.arange(size) - shift) % size]]
  transfers between devices with their start and end apart: 18 -> 26, of which waited for: 18 -> 22; matrix products, arithmetic and copies ran while one was open for 6% -> 7% of each run, Pallas kernels for 0% -> 0%
where the time goes in v1:
time: 1610 us; the launch traced here: 1600 us
  waiting for transfers between devices  1050 us (65%)
  matrix products  242 us (15%)
  other arithmetic  119 us (7%)
  local copies, waits for them, and re-layouts  86.7 us (5%)
  blocking collectives  53.1 us (3%)
  starting transfers between devices  17 us (1%)
  loops' own time  16.4 us (1%)
  between operations  16.1 us (1%)
    reduce_scatter x4, waiting for transfers between devices, row_product(): lax.psum_scatter(jnp.dot(gathered, tile_part, preferred_element_type=jnp....  390 us
    all_gather x4, waiting for transfers between devices, gather_rows(): return lax.all_gather(local_part, 'row', axis=0, tiled=True)  222 us
    reduce_scatter x4, waiting for transfers between devices, col_product(): lax.psum_scatter(jnp.dot(gathered, tile_part, preferred_element_type=jnp....  159 us
    ppermute x8, waiting for transfers between devices, collect(): lower.append(lax.ppermute(lower[-1] if lower else value, axis, pairs))  118 us
    psum x1, waiting for transfers between devices, local(): lax.psum(mod_part.astype(jnp.bfloat16), ('dp', 'col')).astype(jnp.float32)  82.2 us
    psum x1, waiting for transfers between devices, local(): lax.psum(qkv_grad.astype(jnp.bfloat16), 'dp').astype(jnp.float32)  74 us
    dot_general x8, matrix products, masked_scores(): jnp.einsum('sqhd,skhd->shqk', query_part, key_rows, preferred_element_typ...  40.7 us
    dynamic_update_slice x8, local copies, waits for them, and re-layouts, attend_forward(): block_outs, log_totals = lax.map(one_block, offsets)  36 us
  transfers between devices with their start and end apart: 26, of which 22 were waited for; matrix products, arithmetic and copies ran while one was open for 7% of the time, Pallas kernels for 0%

profile of v1, /device:TPU:0, one launch (start us, length us, event | category | flops | bytes accessed | tf_op | source)
XLA Modules:
  0.0 1599.7 jit_solution(3709685258352076811)
XLA Ops:
  18.3 16.0 collective-permute-done
  36.6 9.2 collective-permute-done.1
  64.6 109.9 %reduce-scatter.9.cloned.1.call-done = f32[2048,576]{0,1:T(8,128)} async-done(((f32[4096,576]{0,1:T(8,128)}), f32[2048,576]{0,1:T(8,128)}) %reduce-scatter.9.cloned.1.call-update) | async-done | bytes 4718608 | tf_op jit(solution)/shard_map/reduce_scatter | solution.py:95
  179.6 98.8 %while.27 = (s32[]{:T(128)}, bf16[4,1,512,3,64]{2,4,3,1,0:T(8,128)(2,1)}, f32[4,1,3,512]{3,2,1,0:T(4,128)S(1)}, s32[1,2048]{1,0:T(1,128)S(1)}, s32[4]{0:T(128)S(...) while((s32[]{:T(128)}, ...), condition=%wide.region_8.10_spmd, body=%wide.region_5.9_spmd.sunk | while | flops 844102144 | bytes 50471144 | solution.py:146
  281.3 27.3 %all-gather.5.cloned.1.call-done = bf16[4096,192]{0,1:T(8,128)(2,1)} async-done(((bf16[2048,192]{0,1:T(8,128)(2,1)}), bf16[4096,192]{0,1:T(8,128)(2,1)}) %all-gather.5.cloned.1.call-update) | async-done | bytes 1572880 | tf_op jit(solution)/shard_map/all_gather | solution.py:91
  321.5 17.4 %collective-permute-done.6 = bf16[1024,384]{1,0:T(8,128)(2,1)S(1)} collective-permute-done((bf16[1024,384]{1,0:T(8,128)(2,1)S(1)}, bf16[1024,384]{1,0:T(8,128)(2,1)S(1)}, u32[]{:S(2)}, u32[]{:S(2)}) %collective-permute-start.6) | collective-permute-done | bytes 786464 | tf_op jit(solution)/shard_map/ppermute | solution.py:27
  343.4 24.6 %collective-permute-done.7 = bf16[1024,384]{1,0:T(8,128)(2,1)S(1)} collective-permute-done((bf16[1024,384]{1,0:T(8,128)(2,1)S(1)}, bf16[1024,384]{1,0:T(8,128)(2,1)S(1)}, u32[]{:S(2)}, u32[]{:S(2)}) %collective-permute-start.7) | collective-permute-done | bytes 786464 | tf_op jit(solution)/shard_map/ppermute | solution.py:27
  374.7 9.9 fusion.91
  397.3 14.1 collective-permute-done.3
  430.5 10.1 fusion.89
  441.1 90.4 %reduce-scatter.17.cloned.1.call-done = f32[2048,768]{1,0:T(8,128)} async-done(((f32[4096,768]{1,0:T(8,128)}), f32[2048,768]{1,0:T(8,128)}) %reduce-scatter.17.cloned.1.call-update) | async-done | bytes 6291472 | tf_op jit(solution)/shard_map/reduce_scatter | solution.py:95
  531.4 146.8 %reduce-scatter.13.cloned.1.call-done = f32[2048,768]{1,0:T(8,128)} async-done(((f32[4096,768]{1,0:T(8,128)}), f32[2048,768]{1,0:T(8,128)}) %reduce-scatter.13.cloned.1.call-update) | async-done | bytes 6291472 | tf_op jit(solution)/shard_map/reduce_scatter | solution.py:95
  678.3 9.0 fusion.51
  688.1 79.7 %all-gather.9.cloned.1.call-done = bf16[4096,768]{1,0:T(8,128)(2,1)} async-done(((bf16[2048,768]{1,0:T(8,128)(2,1)}), bf16[4096,768]{1,0:T(8,128)(2,1)}) %all-gather.9.cloned.1.call-update) | async-done | bytes 6291472 | tf_op jit(solution)/shard_map/all_gather | solution.py:91
  767.8 9.5 fusion.92
  777.4 72.3 %all-gather.7.cloned.1.call-done = bf16[4096,768]{1,0:T(8,128)(2,1)} async-done(((bf16[2048,768]{1,0:T(8,128)(2,1)}), bf16[4096,768]{1,0:T(8,128)(2,1)}) %all-gather.7.cloned.1.call-update) | async-done | bytes 6291472 | tf_op jit(solution)/shard_map/all_gather | solution.py:91
  849.7 9.5 fusion.90
  859.3 51.9 %reduce-scatter.19.cloned.1.call-done = f32[1024,384]{1,0:T(8,128)} async-done(((f32[4096,384]{1,0:T(8,128)}), f32[1024,384]{1,0:T(8,128)}) %reduce-scatter.19.cloned.1.call-update) | async-done | bytes 1572880 | tf_op jit(solution)/shard_map/reduce_scatter | solution.py:104
  918.8 53.7 %reduce-scatter.15.cloned.1.call-done = f32[1024,384]{1,0:T(8,128)} async-done(((f32[4096,384]{1,0:T(8,128)}), f32[1024,384]{1,0:T(8,128)}) %reduce-scatter.15.cloned.1.call-update) | async-done | bytes 1572880 | tf_op jit(solution)/shard_map/reduce_scatter | solution.py:104
  978.4 17.4 %collective-permute-done.9 = bf16[1024,384]{1,0:T(8,128)(2,1)S(1)} collective-permute-done((bf16[1024,384]{1,0:T(8,128)(2,1)S(1)}, bf16[1024,384]{1,0:T(8,128)(2,1)S(1)}, u32[]{:S(2)}, u32[]{:S(2)}) %collective-permute-start.9) | collective-permute-done | bytes 786464 | tf_op jit(solution)/shard_map/ppermute | solution.py:27
  995.8 11.4 collective-permute-done.10
  1018.7 43.3 %reduce-scatter.21.cloned.1.call-done = f32[2048,192]{0,1:T(8,128)} async-done(((f32[4096,192]{0,1:T(8,128)}), f32[2048,192]{0,1:T(8,128)}) %reduce-scatter.21.cloned.1.call-update) | async-done | bytes 1572880 | tf_op jit(solution)/shard_map/reduce_scatter | solution.py:95
  1064.4 173.7 %while.28 = (s32[]{:T(128)}, f32[1,2048,3,64]{1,3,2,0:T(8,128)}, f32[1,2048,3,64]{1,3,2,0:T(8,128)}, f32[4,1,512,3,64]{2,0,4,3,1:T(4,128)}, s32[4]{0:T(128)S(1)}...) while((s32[]{:T(128)}, f32[1,2048,3,64]{1,3,2,0:T(8,128)}, ...), condition=%wide.region_25.27_spmd.clone, body=%wide.region_23.26_spmd.clone.sunk | while | flops 2063563264 | bytes 151970208 | solution.py:192
  1098.5 8.6 dynamic_update_slice.19
  1142.2 8.6 dynamic_update_slice.19
  1185.8 8.6 dynamic_update_slice.19
  1229.3 8.6 dynamic_update_slice.19
  1265.6 42.6 %all-gather.11.cloned.1.call-done = bf16[4096,576]{0,1:T(8,128)(2,1)} async-done(((bf16[2048,576]{0,1:T(8,128)(2,1)}), bf16[4096,576]{0,1:T(8,128)(2,1)}) %all-gather.11.cloned.1.call-update) | async-done | bytes 4718608 | tf_op jit(solution)/shard_map/all_gather | solution.py:91
  1326.0 82.2 %all-reduce.9.cloned.1.call-done = bf16[3,384,768]{2,1,0:T(8,128)(2,1)} async-done(((bf16[3,384,768]{2,1,0:T(8,128)(2,1)}), bf16[3,384,768]{2,1,0:T(8,128)(2,1)}) %all-reduce.9.cloned.1.call-update) | async-done | bytes 1769488 | tf_op jit(solution)/shard_map/psum | solution.py:310
  1411.8 74.0 %all-reduce.11.cloned.1.call-done = (bf16[384,3,192]{0,2,1:T(8,128)(2,1)}, bf16[192,384]{1,0:T(8,128)(2,1)}, bf16[384,768]{1,0:T(8,128)(2,1)}, bf16[384,768]{1,0:T(8,128)(2,1)}) async-done(((bf16[384,3,192]{0,2,1:T(8,128)(2,1)}, bf16[192,384]{1,0:T(8,128)(2,1)}, bf16[384,768]{1,0:T(8,128)(2,1)}, bf16[384,768]{1,0:T(8,128)(2,1)}), (bf16[384,3,192]{0,2,1:T(8,128)(2,1)}, bf16[192,384]{1,0:T(8,128)(2,1)}, ...) | async-done | bytes 1769488 | tf_op jit(solution)/shard_map/psum | solution.py:313
  1492.7 53.3 %reduce-scatter.23.cloned.1.call-done = f32[1024,384]{1,0:T(8,128)} async-done(((f32[4096,384]{1,0:T(8,128)}), f32[1024,384]{1,0:T(8,128)}) %reduce-scatter.23.cloned.1.call-update) | async-done | bytes 1572880 | tf_op jit(solution)/shard_map/reduce_scatter | solution.py:104
  1548.3 32.1 %all-reduce.4 = (bf16[384]{0:T(512)(128)(2,1)S(1)}, bf16[384]{0:T(512)(128)(2,1)S(1)}) all-reduce(bf16[384]{0:T(512)(128)(2,1)S(1)} %get-tuple-element.173, bf16[384]{0:T(512)(128)(2,1)S(1)} %get-tuple-element.178), channel_id=1, replica_groups=mesh['dp'=4,'row'=2,'col'=4] {'dp','col'}, use_global_device_ids=true, to_apply=%region_32.34 | all-reduce | flops 768 | bytes 3072 | tf_op jit(solution)/shard_map/psum | solution.py:308
  (342 shorter events, 415.2 us)
Async XLA Ops:
  7.2 309.3 %copy-start = (bf16[3,384,768]{2,1,0:T(8,128)(2,1)S(1)}, bf16[3,384,768]{2,1,0:T(8,128)(2,1)}, u32[]{:S(2)}) copy-start(bf16[3,384,768]{2,1,0:T(8,128)(2,1)} %param.24) | copy-start | bytes 5308420
  7.2 167.3 %reduce-scatter.9.cloned.1.call-start = ((), (), s32[]{:S(2)}) async-start(), calls=%async_computation.8 | async-start | bytes 14155776 | tf_op jit(solution)/shard_map/reduce_scatter | solution.py:95
  16.6 17.7 %collective-permute-start = (bf16[1024,384]{1,0:T(8,128)(2,1)}, bf16[1024,384]{1,0:T(8,128)(2,1)S(1)}, u32[]{:S(2)}, u32[]{:S(2)}) collective-permute-start(bf16[1024,384]{1,0:T(8,128)(2,1)} %fusion.61), channel_id=1, source_target_pairs={{0,1},{1,2},{2,3},{3,0},{4,5},{5,6},{6,7},{7,4},{8,9},{9,10},{10,1... | collective-permute-start | bytes 2359304 | tf_op jit(solution)/shard_map/ppermute | solution.py:27
  16.6 20.0 %collective-permute-start.2 = (bf16[1024,384]{1,0:T(8,128)(2,1)}, bf16[1024,384]{1,0:T(8,128)(2,1)}, u32[]{:S(2)}, u32[]{:S(2)}) collective-permute-start(bf16[1024,384]{1,0:T(8,128)(2,1)} %fusion.61), channel_id=1, source_target_pairs={{1,0},{2,1},{3,2},{0,3},{5,4},{6,5},{7,6},{4,7},{9,8},{10,9},{11,1... | collective-permute-start | bytes 2359304 | tf_op jit(solution)/shard_map/ppermute | solution.py:29
  34.3 11.5 collective-permute-start.1
  60.4 248.2 %all-gather.5.cloned.1.call-start = ((), (), s32[]{:S(2)}) async-start(), calls=%async_computation.9 | async-start | bytes 2359296 | tf_op jit(solution)/shard_map/all_gather | solution.py:91
  64.6 113.5 %copy-start.18 = (f32[2048,32]{0,1:T(8,128)}, f32[2048,32]{0,1:T(8,128)S(1)}, u32[]{:S(2)}) copy-start(f32[2048,32]{0,1:T(8,128)S(1)} %get-tuple-element.267) | copy-start | bytes 786436
  281.3 103.4 %reduce-scatter.11.cloned.1.call-start = ((), (), s32[]{:S(2)}) async-start(), calls=%async_computation.10 | async-start | bytes 7864320 | tf_op jit(solution)/shard_map/reduce_scatter | solution.py:104
  313.9 217.5 %reduce-scatter.17.cloned.1.call-start = ((), (), s32[]{:S(2)}) async-start(), calls=%async_computation.14 | async-start | bytes 18874368 | tf_op jit(solution)/shard_map/reduce_scatter | solution.py:95
  319.7 19.2 %collective-permute-start.6 = (bf16[1024,384]{1,0:T(8,128)(2,1)S(1)}, bf16[1024,384]{1,0:T(8,128)(2,1)S(1)}, u32[]{:S(2)}, u32[]{:S(2)}) collective-permute-start(bf16[1024,384]{1,0:T(8,128)(2,1)S(1)} %fusion.69), channel_id=1, source_target_pairs={{0,1},{1,2},{2,3},{3,0},{4,5},{5,6},{6,7},{7,4},{8,9},{9,10},{10,1... | collective-permute-start | bytes 2359304 | tf_op jit(solution)/shard_map/ppermute | solution.py:27
  319.7 23.7 %collective-permute-start.8 = (bf16[1024,384]{1,0:T(8,128)(2,1)S(1)}, bf16[1024,384]{1,0:T(8,128)(2,1)S(1)}, u32[]{:S(2)}, u32[]{:S(2)}) collective-permute-start(bf16[1024,384]{1,0:T(8,128)(2,1)S(1)} %fusion.69), channel_id=1, source_target_pairs={{1,0},{2,1},{3,2},{0,3},{5,4},{6,5},{7,6},{4,7},{9,8},{10,9},{11,1... | collective-permute-start | bytes 2359304 | tf_op jit(solution)/shard_map/ppermute | solution.py:29
  338.8 29.1 %collective-permute-start.7 = (bf16[1024,384]{1,0:T(8,128)(2,1)S(1)}, bf16[1024,384]{1,0:T(8,128)(2,1)S(1)}, u32[]{:S(2)}, u32[]{:S(2)}) collective-permute-start(bf16[1024,384]{1,0:T(8,128)(2,1)S(1)} %collective-permute-done.6), channel_id=1, source_target_pairs={{0,1},{1,2},{2,3},{3,0},{4,5},{5,6},{6,7},{7,4},{8,9},{9,10},{10,1... | collective-permute-start | bytes 2359304 | tf_op jit(solution)/shard_map/ppermute | solution.py:27
  384.6 293.7 %reduce-scatter.13.cloned.1.call-start = ((), (), s32[]{:S(2)}) async-start(), calls=%async_computation.11 | async-start | bytes 18874368 | tf_op jit(solution)/shard_map/reduce_scatter | solution.py:95
  395.5 15.9 collective-permute-start.3
  395.9 19.8 %collective-permute-start.5 = (bf16[1024,384]{1,0:T(8,128)(2,1)S(1)}, bf16[1024,384]{1,0:T(8,128)(2,1)S(1)}, u32[]{:S(2)}, u32[]{:S(2)}) collective-permute-start(bf16[1024,384]{1,0:T(8,128)(2,1)S(1)} %add_convert_fusion.1), channel_id=1, source_target_pairs={{1,0},{2,1},{3,2},{0,3},{5,4},{6,5},{7,6},{4,7},{9,8},{10,9},{11,1... | collective-permute-start | bytes 2359304 | tf_op jit(solution)/shard_map/ppermute | solution.py:29
  411.4 12.4 collective-permute-start.4
  440.6 327.2 %all-gather.9.cloned.1.call-start = ((), (), s32[]{:S(2)}) async-start(), calls=%async_computation.15 | async-start | bytes 9437184 | tf_op jit(solution)/shard_map/all_gather | solution.py:91
  687.3 162.4 %all-gather.7.cloned.1.call-start = ((), (), s32[]{:S(2)}) async-start(), calls=%async_computation.12 | async-start | bytes 9437184 | tf_op jit(solution)/shard_map/all_gather | solution.py:91
  688.0 223.1 %reduce-scatter.19.cloned.1.call-start = ((), (), s32[]{:S(2)}) async-start(), calls=%async_computation.16 | async-start | bytes 7864320 | tf_op jit(solution)/shard_map/reduce_scatter | solution.py:104
  777.3 195.2 %reduce-scatter.15.cloned.1.call-start = ((), (), s32[]{:S(2)}) async-start(), calls=%async_computation.13 | async-start | bytes 7864320 | tf_op jit(solution)/shard_map/reduce_scatter | solution.py:104
  859.2 202.8 %reduce-scatter.21.cloned.1.call-start = ((), (), s32[]{:S(2)}) async-start(), calls=%async_computation.17 | async-start | bytes 4718592 | tf_op jit(solution)/shard_map/reduce_scatter | solution.py:95
  976.6 19.2 %collective-permute-start.9 = (bf16[1024,384]{1,0:T(8,128)(2,1)S(1)}, bf16[1024,384]{1,0:T(8,128)(2,1)S(1)}, u32[]{:S(2)}, u32[]{:S(2)}) collective-permute-start(bf16[1024,384]{1,0:T(8,128)(2,1)S(1)} %get-tuple-element.257), channel_id=1, source_target_pairs={{0,1},{1,2},{2,3},{3,0},{4,5},{5,6},{6,7},{7,4},{8,9},{9,10},{10,1... | collective-permute-start | bytes 2359304 | tf_op jit(solution)/shard_map/ppermute | solution.py:27
  976.6 19.2 %collective-permute-start.11 = (bf16[1024,384]{1,0:T(8,128)(2,1)S(1)}, bf16[1024,384]{1,0:T(8,128)(2,1)S(1)}, u32[]{:S(2)}, u32[]{:S(2)}) collective-permute-start(bf16[1024,384]{1,0:T(8,128)(2,1)S(1)} %get-tuple-element.257), channel_id=1, source_target_pairs={{1,0},{2,1},{3,2},{0,3},{5,4},{6,5},{7,6},{4,7},{9,8},{10,9},{11,1... | collective-permute-start | bytes 2359304 | tf_op jit(solution)/shard_map/ppermute | solution.py:29
  995.8 11.4 collective-permute-start.10
  1018.6 289.6 %all-gather.11.cloned.1.call-start = ((), (), s32[]{:S(2)}) async-start(), calls=%async_computation.18 | async-start | bytes 7077888 | tf_op jit(solution)/shard_map/all_gather | solution.py:91
  1245.5 162.7 %all-reduce.9.cloned.1.call-start = ((), (), s32[]{:S(2)}) async-start(), calls=%async_computation.20 | async-start | bytes 3538944 | tf_op jit(solution)/shard_map/psum | solution.py:310
  1261.7 224.1 %all-reduce.11.cloned.1.call-start = ((), (), s32[]{:S(2)}) async-start(), calls=%async_computation.21 | async-start | bytes 3538944 | tf_op jit(solution)/shard_map/psum | solution.py:313
  1315.0 231.0 %reduce-scatter.23.cloned.1.call-start = ((), (), s32[]{:S(2)}) async-start(), calls=%async_computation.19 | async-start | bytes 7864320 | tf_op jit(solution)/shard_map/reduce_scatter | solution.py:104
  1411.7 134.3 %copy-start.9 = (bf16[384,1024]{0,1:T(8,128)(2,1)S(1)}, bf16[384,1024]{0,1:T(8,128)(2,1)}, u32[]{:S(2)}) copy-start(bf16[384,1024]{0,1:T(8,128)(2,1)} %copy-done.7) | copy-start | bytes 2359300
  1411.7 134.3 %copy-start.29 = (f32[1024]{0:T(1024)S(1)}, f32[1024]{0:T(1024)}, u32[]{:S(2)}) copy-start(f32[1024]{0:T(1024)} %copy-done.28) | copy-start | bytes 12292
  1411.7 134.3 %copy-start.31 = (f32[1024]{0:T(1024)S(1)}, f32[1024]{0:T(1024)}, u32[]{:S(2)}) copy-start(f32[1024]{0:T(1024)} %copy-done.30) | copy-start | bytes 12292
  1411.7 134.3 %copy-start.33 = (f32[384]{0:T(512)S(1)}, f32[384]{0:T(512)}, u32[]{:S(2)}) copy-start(f32[384]{0:T(512)} %param.18) | copy-start | bytes 4612
  (63 other events, 656.2 us)
Sparse Core Ops, SparseCore 0:
  60.5 113.9 reduce-scatter.8
  281.4 27.1 all-gather.4
  314.1 69.3 reduce-scatter.10
  385.7 145.7 reduce-scatter.16
  533.6 144.6 reduce-scatter.12
  687.4 80.3 all-gather.8
  769.3 80.3 all-gather.6
  852.2 58.8 reduce-scatter.18
  913.7 58.8 reduce-scatter.14
  1018.7 43.2 reduce-scatter.20
  1245.6 62.6 all-gather.10
  1311.6 96.5 all-reduce.8
  1411.4 74.2 all-reduce.10
  1488.1 57.8 reduce-scatter.22
